TPU v7x, 32 devices: a whole 2x2x4 slice. The times are simulated.
32 devices in a mesh: row: 8 (over y, x, core), col: 4 (over z).
Axes of the slice: x: 2, y: 2, z: 4, core: 2. Of those that a mesh axis runs over, the one named last changes fastest.
Arguments:
- image: bfloat16 [512, 512, 512], P('row', 'col'), may hold values from -6 to 6
- w_local: bfloat16 [3, 3, 512, 128], replicated, may hold values from -0.09375 to 0.09375
- w_cross: bfloat16 [3, 3, 128, 384], replicated, may hold values from -0.1875 to 0.1875
- w_spec: bfloat16 [768, 768], replicated, may hold values from -0.21875 to 0.21875
Outputs:
- result: bfloat16 [512, 512, 512], P('row', 'col')
All inputs are finite; a program needn't handle non-finite values.
Results may differ from a plain program's by a relative error of at most 0.0055.
Values may be sent and summed in bfloat16 or wider, within the bound.
A program may use at most 192 MiB of HBM per device.

v0:
```python
import math

import jax
import jax.numpy as jnp
from jax import lax
from jax.sharding import PartitionSpec as P

H = 512
W = 512


def shortened(value):
    return jax.tree.map(lambda a: a.astype(jnp.bfloat16) if a.dtype == jnp.float32 else a, value)


def extended(cells, sides, width):
    for axis, dim in sides:
        count = lax.axis_size(axis)
        ends = count - 1
        head = lax.slice_in_dim(cells, 0, width, axis=dim)
        tail = lax.slice_in_dim(cells, cells.shape[dim] - width, cells.shape[dim], axis=dim)
        cells = jnp.concatenate(
            [
                lax.ppermute(tail, axis, [(i, (i + 1) % count) for i in range(ends)]),
                cells,
                lax.ppermute(head, axis, [((i + 1) % count, i) for i in range(ends)]),
            ],
            axis=dim,
        )
    return cells


def factor_pair(length):
    first = 1
    for divisor in range(1, length + 1):
        if length % divisor == 0 and divisor * divisor <= length:
            first = divisor
    return (first, length // first)


def complex_table(size, sign):
    index = jnp.arange(size, dtype=jnp.int32)
    angle = (jnp.outer(index, index) % size).astype(jnp.float32) * (2.0 * math.pi / size)
    cosine, sine = (jnp.cos(angle), sign * jnp.sin(angle))
    upper = jnp.concatenate([cosine, sine], axis=1)
    lower = jnp.concatenate([-sine, cosine], axis=1)
    return jnp.concatenate([upper, lower], axis=0)


def twiddles(length):
    first, second = factor_pair(length)
    idx_a = jnp.arange(first, dtype=jnp.int32)
    idx_b = jnp.arange(second, dtype=jnp.int32)
    angle_t = (jnp.outer(idx_a, idx_b) % length).astype(jnp.float32) * (2.0 * math.pi / length)
    return (jnp.cos(angle_t)[None, :, :, None], jnp.sin(angle_t)[None, :, :, None])


def contract(form, data, table):
    return jnp.einsum(form, data, table, precision=lax.Precision.HIGHEST)


def forward(real_in, imag_in, length):
    first, second = factor_pair(length)
    cos_t, sin_t = twiddles(length)
    lead, tail = (real_in.shape[0], real_in.shape[2])
    real_in = real_in.reshape(lead, first, second, tail)
    if imag_in is None:
        imag_in = jnp.zeros_like(real_in)
    else:
        imag_in = imag_in.reshape(lead, first, second, tail)
    joined = jnp.concatenate([real_in, imag_in], axis=1)
    one = contract("pnmq,nk->pkmq", joined, complex_table(first, -1.0))
    real_one, imag_one = (one[:, :first], one[:, first:])
    real_two = real_one * cos_t + imag_one * sin_t
    imag_two = imag_one * cos_t - real_one * sin_t
    joined_two = jnp.concatenate([real_two, imag_two], axis=2)
    out = contract("pkmq,ml->plkq", joined_two, complex_table(second, -1.0))
    real_out, imag_out = (out[:, :second], out[:, second:])
    return (real_out.reshape(lead, length, tail), imag_out.reshape(lead, length, tail))


def inverse(real_in, imag_in, length, real_only):
    first, second = factor_pair(length)
    cos_t, sin_t = twiddles(length)
    lead, tail = (real_in.shape[0], real_in.shape[2])
    real_in = real_in.reshape(lead, second, first, tail)
    imag_in = imag_in.reshape(lead, second, first, tail)
    joined = jnp.concatenate([real_in, imag_in], axis=1)
    one = contract("plkq,lm->pkmq", joined, complex_table(second, 1.0))
    real_one, imag_one = (one[:, :, :second], one[:, :, second:])
    real_two = real_one * cos_t - imag_one * sin_t
    imag_two = imag_one * cos_t + real_one * sin_t
    joined_two = jnp.concatenate([real_two, imag_two], axis=1)
    out = contract("pkmq,kn->pnmq", joined_two, complex_table(first, 1.0))
    real_out = out[:, :first].reshape(lead, length, tail)
    if real_only:
        return real_out
    return (real_out, out[:, first:].reshape(lead, length, tail))


def conv_taps(padded, weight, height, width):
    in_chan, out_chan = (weight.shape[2], weight.shape[3])
    beside = jnp.concatenate(
        [padded[:, shift_x : shift_x + width] for shift_x in range(3)], axis=-1
    )
    total = jnp.zeros((height, width, out_chan), jnp.float32)
    for shift_y in range(3):
        flat_weight = weight[shift_y].reshape(3 * in_chan, out_chan)
        total = total + jnp.einsum(
            "hwc,co->hwo",
            beside[shift_y : shift_y + height],
            flat_weight,
            preferred_element_type=jnp.float32,
        )
    return total


def mirrored(values):
    return jnp.roll(jnp.flip(values, 0), 1, 0)


def global_branch(glob, w_spec):
    row_scale = 1.0 / math.sqrt(W)
    col_scale = 1.0 / math.sqrt(H)
    half_w = W // 2
    full_rows = lax.all_to_all(glob, "col", split_axis=0, concat_axis=1, tiled=True)
    real_w, imag_w = forward(full_rows.astype(jnp.float32), None, W)
    real_keep = real_w[:, :half_w]
    imag_keep = jnp.concatenate([real_w[:, half_w : half_w + 1], imag_w[:, 1:half_w]], axis=1)
    packed = (jnp.concatenate([real_keep, imag_keep], axis=-1) * row_scale).astype(jnp.bfloat16)
    columns = lax.all_to_all(packed, ("row", "col"), split_axis=1, concat_axis=0, tiled=True)
    height, bins, spec_chan = columns.shape
    half = spec_chan // 2
    col_data = columns.astype(jnp.float32)
    real_h, imag_h = forward(
        col_data[..., :half].reshape(1, height, bins * half),
        col_data[..., half:].reshape(1, height, bins * half),
        height,
    )
    real_h = real_h.reshape(height, bins, half) * col_scale
    imag_h = imag_h.reshape(height, bins, half) * col_scale
    is_first = lax.axis_index(("row", "col")) == 0
    lead_re, lead_im = (real_h[:, 0], imag_h[:, 0])
    rev_re, rev_im = (mirrored(lead_re), mirrored(lead_im))
    zero_re = jnp.where(is_first, 0.5 * (lead_re + rev_re), lead_re)
    zero_im = jnp.where(is_first, 0.5 * (lead_im - rev_im), lead_im)
    nyq_re = 0.5 * (lead_im + rev_im)
    nyq_im = -0.5 * (lead_re - rev_re)
    real_h = jnp.concatenate([zero_re[:, None], real_h[:, 1:]], axis=1)
    imag_h = jnp.concatenate([zero_im[:, None], imag_h[:, 1:]], axis=1)
    stacked = jnp.concatenate([real_h, imag_h], axis=-1).astype(jnp.bfloat16)
    mixed = jnp.maximum(
        jnp.einsum("hwc,co->hwo", stacked, w_spec, preferred_element_type=jnp.float32), 0.0
    )
    nyq_stack = jnp.concatenate([nyq_re, nyq_im], axis=-1).astype(jnp.bfloat16)
    nyq_mixed = jnp.maximum(jnp.dot(nyq_stack, w_spec, preferred_element_type=jnp.float32), 0.0)
    own_sum = jnp.sum(mixed, axis=(0, 1)) + jnp.where(is_first, jnp.sum(nyq_mixed, axis=0), 0.0)
    totals = lax.psum(own_sum, ("row", "col"))
    mean_value = totals / (H * (half_w + 1))
    centred = mixed - mean_value
    nyq_centred = nyq_mixed - mean_value
    real_b, imag_b = inverse(
        centred[..., :half].reshape(1, height, bins * half),
        centred[..., half:].reshape(1, height, bins * half),
        height,
        False,
    )
    real_b = real_b.reshape(height, bins, half) * col_scale
    imag_b = imag_b.reshape(height, bins, half) * col_scale
    nyq_back = (
        inverse(nyq_centred[:, :half][None], nyq_centred[:, half:][None], height, True)[0]
        * col_scale
    )
    lead_back = jnp.where(is_first, nyq_back, imag_b[:, 0])
    imag_b = jnp.concatenate([lead_back[:, None], imag_b[:, 1:]], axis=1)
    back = jnp.concatenate([real_b, imag_b], axis=-1).astype(jnp.bfloat16)
    row_field = lax.all_to_all(back, ("row", "col"), split_axis=0, concat_axis=1, tiled=True)
    row_field = row_field.astype(jnp.float32)
    freq_re = row_field[..., :half]
    freq_im = row_field[..., half:]
    nyq_row = freq_im[:, 0:1]
    zero_col = jnp.zeros_like(nyq_row)
    full_re = jnp.concatenate([freq_re, nyq_row, jnp.flip(freq_re[:, 1:], 1)], axis=1)
    full_im = jnp.concatenate(
        [zero_col, freq_im[:, 1:], zero_col, -jnp.flip(freq_im[:, 1:], 1)], axis=1
    )
    spatial = inverse(full_re, full_im, W, True) * row_scale
    return lax.all_to_all(
        shortened(spatial), "col", split_axis=1, concat_axis=0, tiled=True
    ).astype(spatial.dtype)


def body(image, w_local, w_cross, w_spec):
    height, width = (image.shape[0], image.shape[1])
    local_chan = w_cross.shape[2]
    padded = extended(image, (("row", 0), ("col", 1)), 1)
    local_out = conv_taps(padded, w_local, height, width)
    cross_out = conv_taps(padded[..., :local_chan], w_cross, height, width)
    spectral = global_branch(image[..., local_chan:], w_spec)
    result = jnp.concatenate([local_out, cross_out + spectral], axis=-1)
    return result.astype(jnp.bfloat16)


def solution(mesh):
    in_specs = (P("row", "col", None), P(), P(), P())
    out_specs = P("row", "col", None)
    return jax.shard_map(body, mesh=mesh, in_specs=in_specs, out_specs=out_specs, check_vma=False)
```

profile of v0, /device:TPU:11, one launch (start us, length us, event | category | flops | bytes accessed | tf_op | source)
XLA Modules:
  0.0 1487.5 jit_solution(12054229031017181042)
XLA Ops:
  12.5 134.1 %all-to-all-done = bf16[64,128,384]{2,1,0:T(8,128)(2,1)} async-done(((bf16[64,128,384]{2,1,0:T(8,128)(2,1)}), bf16[64,128,384]{2,1,0:T(8,128)(2,1)}, u32[]{:S(2)}, u32[]{:S(2)}) %all-to-all-start) | async-done | bytes 6291488 | tf_op jit(solution)/shard_map/all_to_all | solution.py:126
  166.5 14.6 multiply_add_fusion.1
  181.1 14.5 pad_maximum_fusion.1
  195.6 40.0 %fusion.33 = f32[16,64,16,384]{3,1,2,0:T(8,128)} fusion(f32[16,16,64,384]{3,1,2,0:T(8,128)} %pad_maximum_fusion.1, f32[32,32]{0,1:T(8,128)S(1)} %get-tuple-element.48, f32[32,32]{0,1:T(8,128)S(1)} %fusion.119, f32[32,32]{0,1:T(8,128)S(1)} %get-tuple-element.47), kind=kOutput, calls=%fused_computation.58 | convolution fusion | flops 4831850496 | bytes 50343936 | tf_op jit(solution)/shard_map/pkmq,ml->plkq/dot_general | solution.py:59
  235.6 19.7 %fusion.146 = (f32[16,32,16,384]{3,1,2,0:T(8,128)}, f32[16,32,16,384]{3,1,2,0:T(8,128)}) fusion(f32[16,64,16,384]{3,1,2,0:T(8,128)} %fusion.33), kind=kLoop, calls=%fused_computation.208 | loop fusion | bytes 50331648 | tf_op jit(solution)/shard_map/slice | solution.py:78
  255.3 18.9 %copy.158 = f32[16,32,16,384]{3,2,1,0:T(8,128)} copy(f32[16,32,16,384]{3,1,2,0:T(8,128)} %get-tuple-element.9) | data formatting | bytes 25165824 | tf_op jit(solution)/shard_map/slice | solution.py:78
  281.2 19.3 %copy.159 = f32[16,32,16,384]{3,2,1,0:T(8,128)} copy(f32[16,32,16,384]{3,1,2,0:T(8,128)} %get-tuple-element.10) | data formatting | bytes 25165824 | tf_op jit(solution)/shard_map/slice | solution.py:78
  324.5 135.0 %all-to-all-done.1 = bf16[16,256,768]{2,0,1:T(8,128)(2,1)} async-done(((bf16[16,256,768]{2,0,1:T(8,128)(2,1)}), bf16[16,256,768]{2,0,1:T(8,128)(2,1)}, u32[]{:S(2)}, u32[]{:S(2)}) %all-to-all-start.1) | async-done | bytes 6291488 | tf_op jit(solution)/shard_map/all_to_all | solution.py:131
  553.2 25.6 %fusion.42 = f32[1,64,16,3072]{3,1,2,0:T(8,128)} fusion(f32[16,64,3072]{2,0,1:T(8,128)} %maximum_bitcast_fusion.2, f32[32,32]{0,1:T(8,128)S(1)} %get-tuple-element.48, f32[32,32]{0,1:T(8,128)S(1)} %fusion.119, f32[32,32]{0,1:T(8,128)S(1)} %get-tuple-element.47), kind=kOutput, calls=%fused_computation.65 | convolution fusion | flops 2415931392 | bytes 25178112 | tf_op jit(solution)/shard_map/pkmq,ml->plkq/dot_general | solution.py:59
  646.3 39.4 %psum.7 = f32[768]{0:T(1024)S(1)} all-reduce(f32[768]{0:T(1024)S(1)} %select_add_fusion), channel_id=1, replica_groups=mesh['row'=8,'col'=4] {'row','col'}, use_global_device_ids=true, to_apply=%region_2.3 | all-reduce | flops 768 | bytes 6144 | tf_op jit(solution)/shard_map/psum | solution.py:158
  766.5 16.5 %copy.255 = f32[64,16,3072]{2,1,0:T(8,128)} copy(f32[64,16,3072]{2,0,1:T(8,128)} %fusion.17) | data formatting | bytes 25165824 | tf_op jit(solution)/shard_map/plkq,lm->pkmq/dot_general | solution.py:59
  838.4 35.5 %collective-permute-done = bf16[1,128,512]{2,1,0:T(8,128)(2,1)S(1)} collective-permute-done((bf16[1,128,512]{2,1,0:T(8,128)(2,1)S(1)}, bf16[1,128,512]{2,1,0:T(8,128)(2,1)S(1)}, u32[]{:S(2)}, u32[]{:S(2)}) %collective-permute-start) | collective-permute-done | bytes 131104 | tf_op jit(solution)/shard_map/ppermute | solution.py:24
  898.7 70.3 %collective-permute-done.2 = bf16[66,1,512]{2,1,0:T(2,128)(2,1)S(1)} collective-permute-done((bf16[66,1,512]{2,1,0:T(2,128)(2,1)S(1)}, bf16[66,1,512]{2,1,0:T(2,128)(2,1)S(1)}, u32[]{:S(2)}, u32[]{:S(2)}) %collective-permute-start.2) | collective-permute-done | bytes 67616 | tf_op jit(solution)/shard_map/ppermute | solution.py:24
  971.0 16.8 %fusion.29 = (bf16[66,128,512]{2,1,0:T(8,128)(2,1)}, bf16[66,128,512]{2,1,0:T(8,128)(2,1)}) fusion(bf16[66,1,512]{2,1,0:T(2,128)(2,1)S(1)} %collective-permute-done.2, bf16[66,128,512]{2,1,0:T(8,128)(2,1)} %constant_dynamic-update-slice_fusion, bf16[66,1,512]{2,1,0:T(2,128)(2,1)S(1)} %collective-permute-done.3), kind=kLoop, calls=%fused_computation.56 | loop fusion | flops 34603008 | bytes 26087424 | tf_op jit(solution)/shard_map/concatenate | solution.py:22
  1028.3 49.4 %rev.10 = f32[16,255,384]{2,1,0:T(8,128)} reverse(f32[16,255,384]{2,1,0:T(8,128)} %get-tuple-element.15), dimensions={1} | reverse | bytes 12533760 | tf_op jit(solution)/shard_map/jit(_flip)/rev | solution.py:183
  1101.5 49.5 %rev.11 = f32[16,255,384]{2,1,0:T(8,128)} reverse(f32[16,255,384]{2,1,0:T(8,128)} %get-tuple-element.16), dimensions={1} | reverse | bytes 12533760 | tf_op jit(solution)/shard_map/jit(_flip)/rev | solution.py:185
  1173.4 29.4 %fusion = f32[64,16,16,384]{3,0,2,1:T(8,128)} fusion(f32[16,32,16,384]{3,1,2,0:T(8,128)} %copy.193, f32[16,32,16,384]{3,1,2,0:T(8,128)} %copy.192, f32[32,32]{0,1:T(8,128)S(1)} %get-tuple-element.48, f32[32,32]{0,1:T(8,128)S(1)} %copy-done.27, f32[32,32]{0,1:T(8,128)S(1)} %copy-done.26), kind=kOutput, calls=%fused_computation.2 | convolution fusion | flops 4838141952 | bytes 50343936 | tf_op jit(solution)/shard_map/plkq,lm->pkmq/dot_general | solution.py:59
  1202.8 26.8 %copy.254 = f32[64,16,16,384]{3,2,0,1:T(8,128)} copy(f32[64,16,16,384]{3,0,2,1:T(8,128)} %fusion) | data formatting | bytes 50331648 | tf_op jit(solution)/shard_map/plkq,lm->pkmq/dot_general | solution.py:59
  1229.6 19.7 %multiply_subtract_fusion = (f32[16,16,32,384]{3,1,2,0:T(8,128)}, f32[16,16,32,384]{3,1,2,0:T(8,128)}) fusion(f32[16,16,64,384]{3,1,2,0:T(8,128)} %bitcast.188, f32[16,32]{0,1:T(8,128)S(1)} %copy-done.13, f32[16,32]{0,1:T(8,128)S(1)} %copy-done.16), kind=kLoop, calls=%fused_computation.44 | loop fusion | flops 18874368 | bytes 50335744 | tf_op jit(solution)/shard_map/sub | solution.py:91
  1249.4 29.9 %fusion.36 = f32[16,32,32,384]{3,1,2,0:T(8,128)} fusion(f32[16,16,32,384]{3,1,2,0:T(8,128)} %get-tuple-element.6, f32[16,16,32,384]{3,1,2,0:T(8,128)} %get-tuple-element.5, f32[16,16]{0,1:T(8,128)S(1)} %copy-done.25, f32[16,16]{0,1:T(8,128)S(1)} %copy-done.31, f32[16,16]{0,1:T(8,128)S(1)} %copy-done.29), kind=kOutput, calls=%fused_computation.59 | convolution fusion | flops 2422213632 | bytes 50334720 | tf_op jit(solution)/shard_map/pkmq,kn->pnmq/dot_general | solution.py:59
  1304.8 14.8 fusion.145
  1319.6 15.6 %add_convert_fusion = bf16[64,128,128]{1,2,0:T(8,128)(2,1)} fusion(f32[64,128,128]{1,2,0:T(8,128)} %fusion.145, f32[64,128,128]{1,2,0:T(8,128)} %fusion.144, bf16[1536,128,1]{1,0,2:T(8,128)(2,1)S(1)} %bitcast.235, bf16[66,128,512]{2,1,0:T(8,128)(2,1)} %get-tuple-element.24, bf16[66,128,512]{2,1,0:T(8,128)(2,1)} %constant_dynamic-update-slice_fusion, ...), kind=kOutput, calls=%fused_computation.89 | convolution fusion | flops 3302227968 | bytes 36831232 | tf_op jit(solution)/shard_map/hwc,co->hwo/dot_general | solution.py:109
  1358.9 80.3 %all-to-all-done.3 = bf16[16,512,384]{2,0,1:T(8,128)(2,1)} async-done(((bf16[16,512,384]{2,0,1:T(8,128)(2,1)}), bf16[16,512,384]{2,0,1:T(8,128)(2,1)}, u32[]{:S(2)}, u32[]{:S(2)}) %all-to-all-start.3) | async-done | bytes 6291488 | tf_op jit(solution)/shard_map/all_to_all | solution.py:188
  1460.5 19.1 %fusion.23 = bf16[64,128,384]{2,1,0:T(8,128)(2,1)} fusion(f32[4,16,128,384]{3,2,1,0:T(8,128)} %copy.198, f32[64,128,384]{2,1,0:T(8,128)} %fusion.156, f32[64,128,384]{2,1,0:T(8,128)} %fusion.157, bf16[66,128,384]{2,1,0:T(8,128)(2,1)} %copy-done.2, bf16[384,384,1]{1,0,2:T(8,128)(2,1)} %bitcast.232), kind=kOutput, calls=%fused_computation.38 | convolution fusion | flops 2428502016 | bytes 50823168 | tf_op jit(solution)/shard_map/hwc,co->hwo/dot_general | solution.py:109
  (231 shorter events, 552.0 us)
Async XLA Ops:
  0.0 636.5 %copy-start = (bf16[768,768]{1,0:T(8,128)(2,1)S(1)}, bf16[768,768]{1,0:T(8,128)(2,1)}, u32[]{:S(2)}) copy-start(bf16[768,768]{1,0:T(8,128)(2,1)} %param.7) | copy-start | bytes 3538948
  6.8 139.9 %all-to-all-start = ((bf16[64,128,384]{2,1,0:T(8,128)(2,1)}), bf16[64,128,384]{2,1,0:T(8,128)(2,1)}, u32[]{:S(2)}, u32[]{:S(2)}) async-start(bf16[64,128,384]{2,1,0:T(8,128)(2,1)} %slice.253), calls=%async_computation | async-start | bytes 12582912 | tf_op jit(solution)/shard_map/all_to_all | solution.py:126
  12.2 510.4 %copy-start.23 = (f32[16,16]{0,1:T(8,128)}, f32[16,16]{0,1:T(8,128)S(1)}, u32[]{:S(2)}) copy-start(f32[16,16]{0,1:T(8,128)S(1)} %get-tuple-element.44) | copy-start | bytes 3076
  12.4 524.3 %copy-start.11 = (f32[16,32]{0,1:T(8,128)}, f32[16,32]{0,1:T(8,128)S(1)}, u32[]{:S(2)}) copy-start(f32[16,32]{0,1:T(8,128)S(1)} %get-tuple-element.45) | copy-start | bytes 6148
  12.4 524.3 %copy-start.14 = (f32[16,32]{0,1:T(8,128)}, f32[16,32]{0,1:T(8,128)S(1)}, u32[]{:S(2)}) copy-start(f32[16,32]{0,1:T(8,128)S(1)} %get-tuple-element.46) | copy-start | bytes 6148
  313.8 145.7 %all-to-all-start.1 = ((bf16[16,256,768]{2,0,1:T(8,128)(2,1)}), bf16[16,256,768]{2,0,1:T(8,128)(2,1)}, u32[]{:S(2)}, u32[]{:S(2)}) async-start(bf16[16,256,768]{2,0,1:T(8,128)(2,1)} %copy.160), calls=%async_computation.1 | async-start | bytes 12582912 | tf_op jit(solution)/shard_map/all_to_all | solution.py:131
  824.3 177.8 %all-to-all-start.2 = ((bf16[512,8,768]{2,1,0:T(8,128)(2,1)}), bf16[512,8,768]{2,1,0:T(8,128)(2,1)}, u32[]{:S(2)}, u32[]{:S(2)}) async-start(bf16[512,8,768]{2,1,0:T(8,128)(2,1)} %maximum_maximum_fusion), calls=%async_computation.2 | async-start | bytes 12582912 | tf_op jit(solution)/shard_map/all_to_all | solution.py:177
  832.1 41.7 %collective-permute-start = (bf16[1,128,512]{2,1,0:T(8,128)(2,1)S(1)}, bf16[1,128,512]{2,1,0:T(8,128)(2,1)S(1)}, u32[]{:S(2)}, u32[]{:S(2)}) collective-permute-start(bf16[1,128,512]{2,1,0:T(8,128)(2,1)S(1)} %get-tuple-element.28), channel_id=1, source_target_pairs={{0,4},{4,8},{8,12},{12,16},{16,20},{20,24},{24,28},{1,5},{5,9},{9,... | collective-permute-start | bytes 393224 | tf_op jit(solution)/shard_map/ppermute | solution.py:24
  835.4 46.8 %collective-permute-start.1 = (bf16[1,128,512]{2,1,0:T(8,128)(2,1)S(1)}, bf16[1,128,512]{2,1,0:T(8,128)(2,1)S(1)}, u32[]{:S(2)}, u32[]{:S(2)}) collective-permute-start(bf16[1,128,512]{2,1,0:T(8,128)(2,1)S(1)} %get-tuple-element.27), channel_id=1, source_target_pairs={{4,0},{8,4},{12,8},{16,12},{20,16},{24,20},{28,24},{5,1},{9,5},{13... | collective-permute-start | bytes 393224 | tf_op jit(solution)/shard_map/ppermute | solution.py:26
  874.5 20.0 %copy-start.10 = (bf16[3,3,128,384]{3,2,1,0:T(8,128)(2,1)S(1)}, bf16[3,3,128,384]{3,2,1,0:T(8,128)(2,1)}, u32[]{:S(2)}) copy-start(bf16[3,3,128,384]{3,2,1,0:T(8,128)(2,1)} %param.6) | copy-start | bytes 2654212
  884.3 84.6 %collective-permute-start.2 = (bf16[66,1,512]{2,1,0:T(2,128)(2,1)S(1)}, bf16[66,1,512]{2,1,0:T(2,128)(2,1)S(1)}, u32[]{:S(2)}, u32[]{:S(2)}) collective-permute-start(bf16[66,1,512]{2,1,0:T(2,128)(2,1)S(1)} %get-tuple-element.25), channel_id=1, source_target_pairs={{0,1},{1,2},{2,3},{4,5},{5,6},{6,7},{8,9},{9,10},{10,11},{12,13},{... | collective-permute-start | bytes 202760 | tf_op jit(solution)/shard_map/ppermute | solution.py:24
  886.3 84.7 %collective-permute-start.3 = (bf16[66,1,512]{2,1,0:T(2,128)(2,1)S(1)}, bf16[66,1,512]{2,1,0:T(2,128)(2,1)S(1)}, u32[]{:S(2)}, u32[]{:S(2)}) collective-permute-start(bf16[66,1,512]{2,1,0:T(2,128)(2,1)S(1)} %get-tuple-element.26), channel_id=1, source_target_pairs={{1,0},{2,1},{3,2},{5,4},{6,5},{7,6},{9,8},{10,9},{11,10},{13,12},{... | collective-permute-start | bytes 202760 | tf_op jit(solution)/shard_map/ppermute | solution.py:26
  1101.5 53.1 %slice-start = ((s8[6291456]{0:T(1024)(128)(4,1)}), s8[2097152]{0:T(1024)(128)(4,1)S(1)}, s32[]{:S(2)}) async-start(s8[6291456]{0:T(1024)(128)(4,1)} %bitcast.189), calls=%async_computation.4 | async-start | bytes 4194304
  1202.8 26.8 %copy-start.13 = (f32[16,32]{0,1:T(8,128)S(1)}, f32[16,32]{0,1:T(8,128)}, u32[]{:S(2)}) copy-start(f32[16,32]{0,1:T(8,128)} %copy-done.11) | copy-start | bytes 6148
  1202.8 26.8 %copy-start.16 = (f32[16,32]{0,1:T(8,128)S(1)}, f32[16,32]{0,1:T(8,128)}, u32[]{:S(2)}) copy-start(f32[16,32]{0,1:T(8,128)} %copy-done.14) | copy-start | bytes 6148
  1229.6 19.7 %copy-start.25 = (f32[16,16]{0,1:T(8,128)S(1)}, f32[16,16]{0,1:T(8,128)}, u32[]{:S(2)}) copy-start(f32[16,16]{0,1:T(8,128)} %copy-done.23) | copy-start | bytes 3076
  1229.6 19.7 %copy-start.29 = (f32[16,16]{0,1:T(8,128)S(1)}, f32[16,16]{0,1:T(8,128)}, u32[]{:S(2)}) copy-start(f32[16,16]{0,1:T(8,128)} %get-tuple-element.51) | copy-start | bytes 3076
  1229.6 19.7 %copy-start.31 = (f32[16,16]{0,1:T(8,128)S(1)}, f32[16,16]{0,1:T(8,128)}, u32[]{:S(2)}) copy-start(f32[16,16]{0,1:T(8,128)} %get-tuple-element.52) | copy-start | bytes 3076
  1299.2 140.0 %all-to-all-start.3 = ((bf16[16,512,384]{2,0,1:T(8,128)(2,1)}), bf16[16,512,384]{2,0,1:T(8,128)(2,1)}, u32[]{:S(2)}, u32[]{:S(2)}) async-start(bf16[16,512,384]{2,0,1:T(8,128)(2,1)} %copy.196), calls=%async_computation.3 | async-start | bytes 12582912 | tf_op jit(solution)/shard_map/all_to_all | solution.py:188
  1319.6 19.7 %copy-start.3 = (bf16[66,128,128]{2,1,0:T(8,128)(2,1)S(1)}, bf16[66,128,128]{2,1,0:T(8,128)(2,1)}, u32[]{:S(2)}) copy-start(bf16[66,128,128]{2,1,0:T(8,128)(2,1)} %slice.307) | copy-start | bytes 6488068
  1319.6 19.7 %copy-start.18 = (bf16[66,1,512]{2,1,0:T(2,128)(2,1)S(1)}, bf16[66,1,512]{2,1,0:T(2,128)(2,1)}, u32[]{:S(2)}) copy-start(bf16[66,1,512]{2,1,0:T(2,128)(2,1)} %copy-done.17) | copy-start | bytes 202756
  1319.6 19.7 %copy-start.20 = (bf16[66,1,512]{2,1,0:T(2,128)(2,1)S(1)}, bf16[66,1,512]{2,1,0:T(2,128)(2,1)}, u32[]{:S(2)}) copy-start(bf16[66,1,512]{2,1,0:T(2,128)(2,1)} %copy-done.19) | copy-start | bytes 202756
  1460.5 19.1 %copy-start.4 = (bf16[64,128,128]{2,1,0:T(8,128)(2,1)S(1)}, bf16[64,128,128]{2,1,0:T(8,128)(2,1)}, u32[]{:S(2)}) copy-start(bf16[64,128,128]{2,1,0:T(8,128)(2,1)} %copy.199) | copy-start | bytes 6291460
  1460.5 26.7 %copy-start.1 = (bf16[768,768]{1,0:T(8,128)(2,1)S(1)}, bf16[768,768]{1,0:T(8,128)(2,1)}, u32[]{:S(2)}) copy-start(bf16[768,768]{1,0:T(8,128)(2,1)} %param.7) | copy-start | bytes 3538948
  (31 other events, 254.3 us)
where the time goes:
time: 1510 us; the launch traced here: 1490 us
  local copies, waits for them, and re-layouts  486 us (32%)
  waiting for transfers between devices  457 us (30%)
  matrix products  272 us (18%)
  other arithmetic  191 us (13%)
  starting transfers between devices  41.1 us (3%)
  blocking collectives  39.4 us (3%)
    dot_general x10, matrix products, contract(): return jnp.einsum(form, data, table, precision=lax.Precision.HIGHEST)  184 us
    all_to_all x1, waiting for transfers between devices, global_branch(): lax.all_to_all(packed, ('row', 'col'), split_axis=1, concat_axis=0, tiled...  135 us
    all_to_all x1, waiting for transfers between devices, global_branch(): lax.all_to_all(glob, 'col', split_axis=0, concat_axis=1, tiled=True)  134 us
    ppermute x2, waiting for transfers between devices, extended(): lax.ppermute(tail, axis, [(i, (i + 1) % count) for i in range(ends)])  106 us
    all_to_all x1, waiting for transfers between devices, global_branch(): lax.all_to_all(shortened(spatial), 'col', split_axis=1, concat_axis=0, ti...  80.3 us
    dot_general x6, matrix products, conv_taps(): jnp.einsum('hwc,co->hwo', beside[shift_y:shift_y + height], flat_weight,...  77.8 us
    slice x3, local copies, waits for them, and re-layouts, forward(): real_out, imag_out = (out[:, :second], out[:, second:])  57.9 us
    rev x1, local copies, waits for them, and re-layouts, global_branch(): jnp.flip(freq_im[:, 1:], 1)  49.5 us
  transfers between devices with their start and end apart: 8, of which 6 were waited for; matrix products, arithmetic and copies ran while one was open for 7% of the time, Pallas kernels for 0%

commit v1 on v0

v1 whole, which is shorter than its diff:
```python
import jax
import jax.numpy as jnp
import numpy as np
from jax import lax
from jax.sharding import PartitionSpec as P

BOTH = ("row", "col")


def rounded(table):
    return np.asarray(table, np.float32).astype(jnp.bfloat16)


def column_table(height):
    freq = np.arange(height // 2)
    angle = 2.0 * np.pi * (np.outer(freq, np.arange(height)) % height) / height
    table = np.stack([np.cos(angle), -np.sin(angle)], axis=1)
    table[0, 1] = 1.0 - 2.0 * (np.arange(height) % 2)
    return rounded(table.reshape(height, height) / np.sqrt(height))


def width_order(nrow, ncol, width):
    part = width // (nrow * ncol)
    r, c, i = np.meshgrid(np.arange(nrow), np.arange(ncol), np.arange(part), indexing="ij")
    return (c * (width // ncol) + r * part + i).reshape(-1)


def width_tables(order, width, padded):
    half = width // 2
    count = width + 2
    plain = np.concatenate([np.arange(width), [0, half]])
    packed = np.concatenate([np.arange(half + 1), np.arange(half + 1)])
    rows = np.arange(count)
    out = []
    for freq in (plain, packed):
        angle = 2.0 * np.pi * (np.outer(freq, order) % width) / width
        pair = np.zeros((2, padded, width))
        pair[0, :count] = np.cos(angle) / np.sqrt(width)
        pair[1, :count] = np.sin(angle) / np.sqrt(width)
        out.append(rounded(pair))
    sign = np.where(rows <= half, 1.0, -1.0)
    scale_plain = np.where(np.isin(rows, [0, half, width, width + 1]), 1.0, 2.0)
    scale_packed = np.where(np.isin(packed, [0, half]), 1.0, 2.0)
    extra = padded - count
    pad = lambda v: np.pad(v, (0, extra))
    upper = pad((rows <= half).astype(np.float64))
    lower = pad((rows > half).astype(np.float64))
    return out[0], out[1], pad(sign), upper, lower, pad(scale_plain), pad(scale_packed)


def assembled(pair, blocks, xp):
    cosine, sine = pair[0], pair[1]
    pick = {"c": cosine, "s": sine}
    lines = []
    for line in blocks:
        lines.append(xp.concatenate([pick[k] * v[:, None] for k, v in line], axis=1))
    return xp.concatenate(lines, axis=0)


def extended(cells, sides, width):
    for axis, dim in sides:
        count = lax.axis_size(axis)
        ends = count - 1
        head = lax.slice_in_dim(cells, 0, width, axis=dim)
        tail = lax.slice_in_dim(cells, cells.shape[dim] - width, cells.shape[dim], axis=dim)
        cells = jnp.concatenate(
            [
                lax.ppermute(tail, axis, [(i, (i + 1) % count) for i in range(ends)]),
                cells,
                lax.ppermute(head, axis, [((i + 1) % count, i) for i in range(ends)]),
            ],
            axis=dim,
        )
    return cells


def conv(padded, weight):
    return lax.conv_general_dilated(
        padded[None],
        weight,
        (1, 1),
        "VALID",
        dimension_numbers=("NHWC", "HWIO", "NHWC"),
        preferred_element_type=jnp.float32,
    )[0]


def product(form, left, right):
    return jnp.einsum(form, left, right, preferred_element_type=jnp.float32)


def global_branch(glob, w_spec):
    nrow, ncol = lax.axis_size("row"), lax.axis_size("col")
    count = nrow * ncol
    height, width, ch = glob.shape[0] * nrow, glob.shape[1] * ncol, glob.shape[2]
    bins = height // (2 * count)
    padded = -(-(width + 2) // 16) * 16

    columns = lax.all_to_all(glob, "row", split_axis=1, concat_axis=0, tiled=True)

    col_np = column_table(height)
    plain_np, packed_np, sign, upper, lower, scale_plain, scale_packed = width_tables(
        width_order(nrow, ncol, width), width, padded
    )
    ones = np.ones_like(sign)
    plain_form = ((("c", ones), ("s", ones)), (("s", -sign), ("c", sign)))
    packed_form = ((("c", upper), ("c", lower)), (("s", -upper), ("s", -lower)))

    def row_sums(pair, form, scale):
        table = assembled(pair.astype(np.float64), form, np) * np.tile(scale, 2)[:, None]
        return np.stack([table[:padded].sum(0), table[padded:].sum(0)], axis=1).astype(np.float32)

    def cast_form(form):
        return [[(k, jnp.asarray(rounded(v))) for k, v in line] for line in form]

    col_table = jnp.asarray(col_np)
    is_first = lax.axis_index(BOTH) == 0
    special = (is_first & (jnp.arange(bins) == 0))[:, None, None]
    table = jnp.where(
        special,
        assembled(jnp.asarray(packed_np), cast_form(packed_form), jnp)[None],
        assembled(jnp.asarray(plain_np), cast_form(plain_form), jnp)[None],
    )
    scale = jnp.where(
        special,
        jnp.asarray(scale_packed, jnp.float32)[None, :, None],
        jnp.asarray(scale_plain, jnp.float32)[None, :, None],
    )
    sums = jnp.where(
        special,
        jnp.asarray(row_sums(packed_np, packed_form, scale_packed))[None],
        jnp.asarray(row_sums(plain_np, plain_form, scale_plain))[None],
    )

    field = product("uh,hwc->uwc", col_table, columns).astype(jnp.bfloat16)
    lines = lax.all_to_all(field, BOTH, split_axis=0, concat_axis=1, tiled=True)
    lines = lines.reshape(bins, 2 * width, ch)
    spectrum = product("bmk,bkc->bmc", table, lines).astype(jnp.bfloat16)
    stacked = jnp.concatenate([spectrum[:, :padded], spectrum[:, padded:]], axis=-1)
    mixed = jnp.maximum(product("bvc,co->bvo", stacked, w_spec), 0.0)
    own_sum = jnp.sum(mixed, axis=(0, 1))
    every = lax.all_to_all(
        jnp.broadcast_to(own_sum[None], (count, 2 * ch)), BOTH, split_axis=0, concat_axis=0, tiled=True
    )
    mean = jnp.sum(every, axis=0) / (height * (width // 2 + 1))
    scaled = (mixed * scale).astype(jnp.bfloat16)
    scaled = jnp.concatenate([scaled[..., :ch], scaled[..., ch:]], axis=1)
    offset = sums[:, :, :1] * mean[:ch] + sums[:, :, 1:] * mean[ch:]
    inverted = (product("bkm,bkc->bmc", table, scaled) - offset).astype(jnp.bfloat16)
    inverted = inverted.reshape(2 * bins, width, ch)
    back = lax.all_to_all(inverted, BOTH, split_axis=1, concat_axis=0, tiled=True)
    rows = product("uh,uwc->hwc", col_table, back).astype(jnp.bfloat16)
    return lax.all_to_all(rows, "row", split_axis=0, concat_axis=1, tiled=True)


def body(image, w_local, w_cross, w_spec):
    local_chan = w_cross.shape[2]
    spectral = global_branch(image[..., local_chan:], w_spec)
    padded = extended(image, (("row", 0), ("col", 1)), 1)
    local_out = conv(padded, w_local)
    cross_out = conv(padded[..., :local_chan], w_cross)
    result = jnp.concatenate(
        [local_out.astype(jnp.bfloat16), (cross_out + spectral).astype(jnp.bfloat16)], axis=-1
    )
    return result


def solution(mesh):
    in_specs = (P("row", "col", None), P(), P(), P())
    out_specs = P("row", "col", None)
    return jax.shard_map(body, mesh=mesh, in_specs=in_specs, out_specs=out_specs, check_vma=False)
```

time: 1510 us -> 632 us (0.42); the launches traced: 1490 us -> 627 us
  local copies, waits for them, and re-layouts: 486 us -> 120 us
  waiting for transfers between devices: 457 us -> 258 us
  matrix products: 272 us -> 78.8 us
  other arithmetic: 191 us -> 52.9 us
  blocking collectives: 39.4 us -> 74.5 us
    dot_general x18 -> x5, matrix products: 272 us -> 41.7 us  [product(): return jnp.einsum(form, left, right, preferred_element_type=jnp.float32)]
    all_to_all x4, waiting for transfers between devices: 349 us -> 137 us  [the longest x1 137 us: global_branch(): lines = lax.all_to_all(field, BOTH, split_axis=0, concat_axis=1, tiled=True)]
    slice x30 -> x3, local copies, waits for them, and re-layouts: 150 us -> 6.96 us  [the longest x1 6.31 us: global_branch(): scaled = jnp.concatenate([scaled[..., :ch], scaled[..., ch:]], axis=1)]
    rev x2 -> x0, local copies, waits for them, and re-layouts: 98.9 us -> none  [the longest x1 49.5 us: global_branch(): jnp.flip(freq_im[:, 1:], 1)]
    all_to_all x0 -> x1, blocking collectives: none -> 74.5 us  [global_branch(): lax.all_to_all(glob, 'row', split_axis=1, concat_axis=0, tiled=True)]
    another operation x13 -> x0, local copies, waits for them, and re-layouts: 70.7 us -> none  [the longest x3 16.9 us: inverse(): real_in = real_in.reshape(lead, second, first, tail)]
    dot_general x2 -> x0, local copies, waits for them, and re-layouts: 43.3 us -> none  [contract(): return jnp.einsum(form, data, table, precision=lax.Precision.HIGHEST)]
    concatenate x6 -> x1, other arithmetic: 47.9 us -> 7.76 us  [body(): jnp.concatenate([local_out.astype(jnp.bfloat16), (cross_out + spectral).a...]
  transfers between devices with their start and end apart: 8 -> 8, of which waited for: 6 -> 4; matrix products, arithmetic and copies ran while one was open for 7% -> 17% of each run, Pallas kernels for 0% -> 0%
where the time goes in v1:
time: 632 us; the launch traced here: 627 us
  waiting for transfers between devices  258 us (41%)
  local copies, waits for them, and re-layouts  120 us (19%)
  matrix products  78.8 us (12%)
  blocking collectives  74.5 us (12%)
  other arithmetic  52.9 us (8%)
  starting transfers between devices  43 us (7%)
    all_to_all x1, waiting for transfers between devices, global_branch(): lines = lax.all_to_all(field, BOTH, split_axis=0, concat_axis=1, tiled=True)  137 us
    ppermute x2, waiting for transfers between devices, extended(): lax.ppermute(tail, axis, [(i, (i + 1) % count) for i in range(ends)])  118 us
    all_to_all x1, blocking collectives, global_branch(): lax.all_to_all(glob, 'row', split_axis=1, concat_axis=0, tiled=True)  74.5 us
    dot_general x5, matrix products, product(): return jnp.einsum(form, left, right, preferred_element_type=jnp.float32)  41.7 us
    conv_general_dilated x2, matrix products, conv(): lax.conv_general_dilated(padded[None], weight, (1, 1), 'VALID', dimension...  37.2 us
    conv_general_dilated x5, local copies, waits for them, and re-layouts, conv(): lax.conv_general_dilated(padded[None], weight, (1, 1), 'VALID', dimension...  23.4 us
    unnamed x29, local copies, waits for them, and re-layouts  13.2 us
    convert_element_type x1, local copies, waits for them, and re-layouts, body(): cross_out + spectral  12.8 us
  transfers between devices with their start and end apart: 8, of which 4 were waited for; matrix products, arithmetic and copies ran while one was open for 17% of the time, Pallas kernels for 0%

profile of v1, /device:TPU:11, one launch (start us, length us, event | category | flops | bytes accessed | tf_op | source)
XLA Modules:
  0.0 627.0 jit_solution(2966774456978388852)
XLA Ops:
  0.0 11.6 %copy.97 = bf16[64,128,512]{2,0,1:T(8,128)(2,1)} copy(bf16[64,128,512]{2,1,0:T(8,128)(2,1)} %param.19) | data formatting | bytes 16777216 | tf_op args[0]
  14.4 74.5 %all_to_all.66 = bf16[64,128,384]{2,0,1:T(8,128)(2,1)S(1)} all-to-all(bf16[64,128,384]{2,0,1:T(8,128)(2,1)S(1)} %slice-done), channel_id=1, replica_groups=mesh['row'=8,'col'=4] {'row'}, dimensions={1} | all-to-all | bytes 12582912 | tf_op jit(solution)/shard_map/all_to_all | solution.py:99
  96.8 6.4 %copy.108 = bf16[512,16,384]{2,1,0:T(8,128)(2,1)} copy(bf16[512,16,384]{2,0,1:T(8,128)(2,1)S(1)} %fusion.40) | data formatting | bytes 12582912 | tf_op jit(solution)/shard_map/convert_element_type | solution.py:135
  109.6 137.3 %all-to-all-done.1 = bf16[512,16,384]{2,1,0:T(8,128)(2,1)} async-done(((bf16[512,16,384]{2,1,0:T(8,128)(2,1)}), bf16[512,16,384]{2,1,0:T(8,128)(2,1)}, u32[]{:S(2)}, u32[]{:S(2)}) %all-to-all-start.1) | async-done | bytes 6291488 | tf_op jit(solution)/shard_map/all_to_all | solution.py:136
  250.8 9.8 %fusion.20 = bf16[8,1056,384]{2,1,0:T(8,128)(2,1)S(1)} fusion(bf16[8,1024,384]{2,1,0:T(8,128)(2,1)S(1)} %bitcast.62, pred[8]{0:T(512)(128)(4,1)S(1)} %compare_and_fusion, bf16[1056,1024]{1,0:T(8,128)(2,1)S(1)} %copy-done.9, bf16[1056,1024]{1,0:T(8,128)(2,1)S(1)} %copy-done.10), kind=kOutput, calls=%fused_computation.28 | convolution fusion | flops 6655672320 | bytes 17104904 | tf_op jit(solution)/shard_map/bmk,bkc->bmc/dot_general | solution.py:89
  261.3 7.1 %maximum_reduce_fusion = (f32[768]{0:T(1024)S(1)}, bf16[8,528,768]{2,1,0:T(8,128)(2,1)}) fusion(f32[8,528]{1,0:T(8,128)S(1)} %broadcast_select_fusion.1, bf16[768,768]{1,0:T(8,128)(2,1)S(1)} %copy-done, bf16[8,528,384]{2,1,0:T(8,128)(2,1)S(1)} %get-tuple-element.14, bf16[8,528,384]{2,1,0:T(8,128)(2,1)S(1)} %get-tuple-element.13), kind=kOutput, calls=%fused_computation.14 | convolution fusion | flops 5008784384 | bytes 14175744 | tf_op jit(solution)/shard_map/bvc,co->bvo/dot_general | solution.py:89
  281.9 14.6 %subtract_convert_fusion = bf16[8,1024,384]{2,1,0:T(8,128)(2,1)S(1)} fusion(bf16[8,528,384]{2,1,0:T(8,128)(2,1)} %get-tuple-element.12, bf16[8,528,384]{2,1,0:T(8,128)(2,1)} %get-tuple-element.11, pred[8]{0:T(512)(128)(4,1)S(1)} %compare_and_fusion, bf16[1056,1024]{1,0:T(8,128)(2,1)S(1)} %copy-done.9, bf16[1056,1024]{1,0:T(8,128)(2,1)} %constant.82, ...), kind=kOutput, calls=%fused_computation.13 | convolution fusion | flops 6681133056 | bytes 17173512 | tf_op jit(solution)/shard_map/bkm,bkc->bmc/dot_general | solution.py:89
  315.0 36.4 %collective-permute-done = bf16[1,128,512]{2,1,0:T(8,128)(2,1)S(1)} collective-permute-done((bf16[1,128,512]{2,1,0:T(8,128)(2,1)S(1)}, bf16[1,128,512]{2,1,0:T(8,128)(2,1)S(1)}, u32[]{:S(2)}, u32[]{:S(2)}) %collective-permute-start) | collective-permute-done | bytes 131104 | tf_op jit(solution)/shard_map/ppermute | solution.py:68
  354.8 8.7 %collective-permute-start.3 = (bf16[66,1,512]{2,0,1:T(8,128)(2,1)S(1)}, bf16[66,1,512]{2,0,1:T(8,128)(2,1)S(1)}, u32[]{:S(2)}, u32[]{:S(2)}) collective-permute-start(bf16[66,1,512]{2,0,1:T(8,128)(2,1)S(1)} %get-tuple-element.8), channel_id=1, source_target_pairs={{1,0},{2,1},{3,2},{5,4},{6,5},{7,6},{9,8},{10,9},{11,10},{13,12},{... | collective-permute-start | bytes 202760 | tf_op jit(solution)/shard_map/ppermute | solution.py:70
  363.5 81.9 %collective-permute-done.2 = bf16[66,1,512]{2,0,1:T(8,128)(2,1)S(1)} collective-permute-done((bf16[66,1,512]{2,0,1:T(8,128)(2,1)S(1)}, bf16[66,1,512]{2,0,1:T(8,128)(2,1)S(1)}, u32[]{:S(2)}, u32[]{:S(2)}) %collective-permute-start.2) | collective-permute-done | bytes 67616 | tf_op jit(solution)/shard_map/ppermute | solution.py:68
  447.4 11.5 %fusion.72 = bf16[66,1,130,512]{3,0,2,1:T(8,128)(2,1)} fusion(bf16[66,1,512]{2,0,1:T(8,128)(2,1)S(1)} %collective-permute-done.3, bf16[1,128,512]{2,0,1:T(2,128)(2,1)S(1)} %copy.98, bf16[64,128,512]{2,0,1:T(8,128)(2,1)} %copy.97, bf16[1,128,512]{2,0,1:T(2,128)(2,1)S(1)} %copy.96, bf16[66,1,512]{2,0,1:T(8,128)(2,1)S(1)} %collective-permute-done.2), kind=kLoop, calls=%fused_computation.76 | loop fusion | flops 43929600 | bytes 17571840 | tf_op jit(solution)/shard_map/broadcast_in_dim | solution.py:79
  469.3 9.1 %copy.114 = bf16[512,16,384]{2,1,0:T(8,128)(2,1)} copy(bf16[512,16,384]{0,2,1:T(8,128)(2,1)} %convert_bitcast_fusion.1) | data formatting | bytes 12582912 | tf_op jit(solution)/shard_map/convert_element_type | solution.py:152
  478.3 8.7 %all-to-all-start.4 = ((bf16[512,16,384]{2,1,0:T(8,128)(2,1)}), bf16[512,16,384]{2,1,0:T(8,128)(2,1)}, u32[]{:S(2)}, u32[]{:S(2)}) async-start(bf16[512,16,384]{2,1,0:T(8,128)(2,1)} %copy.114), calls=%async_computation.4 | async-start | bytes 12582912 | tf_op jit(solution)/shard_map/all_to_all | solution.py:153
  487.0 11.5 %pad_maximum_fusion = bf16[66,130,512]{2,0,1:T(8,128)(2,1)} fusion(bf16[66,1,512]{2,0,1:T(8,128)(2,1)S(1)} %collective-permute-done.3, bf16[1,128,512]{2,0,1:T(2,128)(2,1)S(1)} %copy.98, bf16[64,128,512]{2,0,1:T(8,128)(2,1)} %copy.97, bf16[1,128,512]{2,0,1:T(2,128)(2,1)S(1)} %copy.96, bf16[66,1,512]{2,0,1:T(8,128)(2,1)S(1)} %collective-permute-done.2), kind=kLoop, calls=%fused_computation.21 | loop fusion | flops 43929600 | bytes 17571840 | tf_op jit(solution)/shard_map/concatenate | solution.py:66
  498.5 8.2 %pad = bf16[66,1,136,512]{3,0,2,1:T(8,128)(2,1)} pad(bf16[66,1,130,512]{3,0,2,1:T(8,128)(2,1)} %fusion.72, bf16[]{:T(256)} %constant.62), padding=0_0x0_0x0_6x0_0 | pad | bytes 17977346 | tf_op jit(solution)/shard_map/broadcast_in_dim | solution.py:79
  506.7 10.6 %copy.100 = bf16[66,1,8,17,512]{4,2,3,0,1:T(8,128)(2,1)} copy(bf16[66,1,8,17,512]{4,0,3,2,1:T(8,128)(2,1)} %bitcast.56) | data formatting | bytes 18382848 | tf_op jit(solution)/shard_map/conv_general_dilated | solution.py:78
  522.1 21.6 %select_convert_fusion = bf16[64,8,17,128]{3,1,2,0:T(8,128)(2,1)S(1)} fusion(pred[8,17]{0,1:T(8,128)(4,1)S(1)} %copy-done.13, bf16[3,3,512,128]{3,2,1,0:T(8,128)(2,1)S(1)} %copy-done.8, bf16[66,1,7,2,512]{4,2,3,0,1:T(8,128)(2,1)S(1)} %slice.76, bf16[66,1,8,17,512]{4,2,3,0,1:T(8,128)(2,1)S(1)} %copy-done.2), kind=kOutput, calls=%fused_computation.44 | convolution fusion | flops 10300702720 | bytes 13545608 | tf_op jit(solution)/shard_map/conv_general_dilated | solution.py:78
  544.4 15.5 %convolution_select_fusion = f32[64,8,17,384]{3,1,2,0:T(8,128)} fusion(bf16[3,3,128,384]{3,2,1,0:T(8,128)(2,1)} %param.21, pred[8,17]{0,1:T(8,128)(4,1)S(1)} %copy-done.13, bf16[66,1,7,2,128]{4,2,3,0,1:T(8,128)(2,1)S(1)} %slice.79, bf16[66,1,8,17,128]{4,2,3,0,1:T(8,128)(2,1)S(1)} %copy.103), kind=kOutput, calls=%fused_computation.22 | convolution fusion | flops 7711789056 | bytes 16788616 | tf_op jit(solution)/shard_map/conv_general_dilated | solution.py:78
  559.9 12.2 %copy.104 = f32[64,8,17,384]{3,0,2,1:T(8,128)} copy(f32[64,8,17,384]{3,1,2,0:T(8,128)} %convolution_select_fusion) | data formatting | bytes 26738688 | tf_op jit(solution)/shard_map/conv_general_dilated | solution.py:78
  573.6 8.4 %convert_bitcast_fusion = f32[64,8,16,384]{3,2,0,1:T(8,128)} fusion(bf16[8,64,16,384]{3,2,1,0:T(8,128)(2,1)} %bitcast.26), kind=kLoop, calls=%fused_computation.12 | loop fusion | flops 3145728 | bytes 18874368 | tf_op jit(solution)/shard_map/convert_element_type | solution.py:163
  582.0 12.8 %copy.115 = f32[64,8,16,384]{3,0,2,1:T(8,128)} copy(f32[64,8,16,384]{3,2,0,1:T(8,128)} %convert_bitcast_fusion) | data formatting | bytes 25165824 | tf_op jit(solution)/shard_map/convert_element_type | solution.py:163
  594.8 12.6 %fusion.8 = bf16[64,128,384]{2,0,1:T(8,128)(2,1)} fusion(f32[64,1,136,384]{3,0,2,1:T(8,128)} %bitcast.55, f32[64,8,16,384]{3,0,2,1:T(8,128)} %copy.115), kind=kLoop, calls=%fused_computation.11 | loop fusion | flops 6291456 | bytes 31457280 | tf_op jit(solution)/shard_map/convert_element_type | solution.py:163
  607.4 7.8 %pad_maximum_fusion.1 = bf16[64,128,512]{2,0,1:T(8,128)(2,1)} fusion(bf16[64,128,384]{2,0,1:T(8,128)(2,1)} %fusion.8, bf16[64,128,128]{2,0,1:T(8,128)(2,1)S(1)} %copy-done.3), kind=kLoop, calls=%fused_computation.27 | loop fusion | flops 16777216 | bytes 16777216 | tf_op jit(solution)/shard_map/concatenate | solution.py:162
  615.2 11.5 %copy.116 = bf16[64,128,512]{2,1,0:T(8,128)(2,1)} copy(bf16[64,128,512]{2,0,1:T(8,128)(2,1)} %pad_maximum_fusion.1) | data formatting | bytes 16777216 | tf_op jit(solution)/shard_map/concatenate | solution.py:162
  (68 shorter events, 76.1 us)
Async XLA Ops:
  0.0 261.2 %copy-start = (bf16[768,768]{1,0:T(8,128)(2,1)S(1)}, bf16[768,768]{1,0:T(8,128)(2,1)}, u32[]{:S(2)}) copy-start(bf16[768,768]{1,0:T(8,128)(2,1)} %param.22) | copy-start | bytes 3538948
  11.6 2.8 slice-start
  88.9 3.8 copy-start.12
  103.2 6.2 copy-start.6
  103.2 6.2 copy-start.7
  103.2 6.3 %copy-start.4 = (f32[1024,2]{0,1:T(2,128)S(1)}, f32[1024,2]{0,1:T(2,128)}, u32[]{:S(2)}) copy-start(f32[1024,2]{0,1:T(2,128)} %constant.61.clone) | copy-start | bytes 24580
  103.2 6.3 %copy-start.5 = (f32[1024,2]{0,1:T(2,128)S(1)}, f32[1024,2]{0,1:T(2,128)}, u32[]{:S(2)}) copy-start(f32[1024,2]{0,1:T(2,128)} %constant.60.clone) | copy-start | bytes 24580
  103.2 143.7 %all-to-all-start.1 = ((bf16[512,16,384]{2,1,0:T(8,128)(2,1)}), bf16[512,16,384]{2,1,0:T(8,128)(2,1)}, u32[]{:S(2)}, u32[]{:S(2)}) async-start(bf16[512,16,384]{2,1,0:T(8,128)(2,1)} %copy.108), calls=%async_computation.1 | async-start | bytes 12582912 | tf_op jit(solution)/shard_map/all_to_all | solution.py:136
  109.4 141.4 %copy-start.9 = (bf16[1056,1024]{1,0:T(8,128)(2,1)S(1)}, bf16[1056,1024]{1,0:T(8,128)(2,1)}, u32[]{:S(2)}) copy-start(bf16[1056,1024]{1,0:T(8,128)(2,1)} %constant.91) | copy-start | bytes 6488068
  246.9 3.9 copy-start.10
  269.1 12.7 %all-to-all-start.2 = ((f32[32,1,768]{2,1,0:T(1,128)}), f32[32,1,768]{2,1,0:T(1,128)S(1)}, u32[]{:S(2)}, u32[]{:S(2)}) async-start(f32[32,1,768]{2,1,0:T(1,128)} %broadcast_in_dim.112), calls=%async_computation.2 | async-start | bytes 196608 | tf_op jit(solution)/shard_map/all_to_all | solution.py:142
  302.9 156.1 %all-to-all-start.3 = ((bf16[16,512,384]{2,0,1:T(8,128)(2,1)}), bf16[16,512,384]{2,0,1:T(8,128)(2,1)}, u32[]{:S(2)}, u32[]{:S(2)}) async-start(bf16[16,512,384]{2,0,1:T(8,128)(2,1)} %copy.111), calls=%async_computation.3 | async-start | bytes 12582912 | tf_op jit(solution)/shard_map/all_to_all | solution.py:151
  309.7 41.7 %collective-permute-start = (bf16[1,128,512]{2,1,0:T(8,128)(2,1)S(1)}, bf16[1,128,512]{2,1,0:T(8,128)(2,1)S(1)}, u32[]{:S(2)}, u32[]{:S(2)}) collective-permute-start(bf16[1,128,512]{2,1,0:T(8,128)(2,1)S(1)} %get-tuple-element.9), channel_id=1, source_target_pairs={{0,4},{4,8},{8,12},{12,16},{16,20},{20,24},{24,28},{1,5},{5,9},{9,... | collective-permute-start | bytes 393224 | tf_op jit(solution)/shard_map/ppermute | solution.py:68
  313.1 38.6 %collective-permute-start.1 = (bf16[1,128,512]{2,1,0:T(8,128)(2,1)S(1)}, bf16[1,128,512]{2,1,0:T(8,128)(2,1)S(1)}, u32[]{:S(2)}, u32[]{:S(2)}) collective-permute-start(bf16[1,128,512]{2,1,0:T(8,128)(2,1)S(1)} %get-tuple-element.10), channel_id=1, source_target_pairs={{4,0},{8,4},{12,8},{16,12},{20,16},{24,20},{28,24},{5,1},{9,5},{13... | collective-permute-start | bytes 393224 | tf_op jit(solution)/shard_map/ppermute | solution.py:70
  352.8 92.6 %collective-permute-start.2 = (bf16[66,1,512]{2,0,1:T(8,128)(2,1)S(1)}, bf16[66,1,512]{2,0,1:T(8,128)(2,1)S(1)}, u32[]{:S(2)}, u32[]{:S(2)}) collective-permute-start(bf16[66,1,512]{2,0,1:T(8,128)(2,1)S(1)} %get-tuple-element.7), channel_id=1, source_target_pairs={{0,1},{1,2},{2,3},{4,5},{5,6},{6,7},{8,9},{9,10},{10,11},{12,13},{... | collective-permute-start | bytes 202760 | tf_op jit(solution)/shard_map/ppermute | solution.py:68
  354.8 92.7 %collective-permute-start.3 = (bf16[66,1,512]{2,0,1:T(8,128)(2,1)S(1)}, bf16[66,1,512]{2,0,1:T(8,128)(2,1)S(1)}, u32[]{:S(2)}, u32[]{:S(2)}) collective-permute-start(bf16[66,1,512]{2,0,1:T(8,128)(2,1)S(1)} %get-tuple-element.8), channel_id=1, source_target_pairs={{1,0},{2,1},{3,2},{5,4},{6,5},{7,6},{9,8},{10,9},{11,10},{13,12},{... | collective-permute-start | bytes 202760 | tf_op jit(solution)/shard_map/ppermute | solution.py:70
  458.9 4.4 copy-start.11
  478.3 95.2 %all-to-all-start.4 = ((bf16[512,16,384]{2,1,0:T(8,128)(2,1)}), bf16[512,16,384]{2,1,0:T(8,128)(2,1)}, u32[]{:S(2)}, u32[]{:S(2)}) async-start(bf16[512,16,384]{2,1,0:T(8,128)(2,1)} %copy.114), calls=%async_computation.4 | async-start | bytes 12582912 | tf_op jit(solution)/shard_map/all_to_all | solution.py:153
  517.3 4.3 copy-start.2
  519.5 2.6 copy-start.8
  519.5 2.6 copy-start.13
  594.8 12.6 %copy-start.3 = (bf16[64,128,128]{2,0,1:T(8,128)(2,1)S(1)}, bf16[64,128,128]{2,0,1:T(8,128)(2,1)}, u32[]{:S(2)}) copy-start(bf16[64,128,128]{2,0,1:T(8,128)(2,1)} %slice_bitcast_fusion.2) | copy-start | bytes 6291460
  607.4 19.3 %copy-start.1 = (bf16[768,768]{1,0:T(8,128)(2,1)S(1)}, bf16[768,768]{1,0:T(8,128)(2,1)}, u32[]{:S(2)}) copy-start(bf16[768,768]{1,0:T(8,128)(2,1)} %param.22) | copy-start | bytes 3538948
